TPU v7x, 32 devices: a whole 2x2x4 slice. The times are simulated.
32 devices in a mesh: gx: 4 (over z), gy: 2 (over y), gz: 4 (over x, core).
Axes of the slice: x: 2, y: 2, z: 4, core: 2. Of those that a mesh axis runs over, the one named last changes fastest.
Arguments:
- adjoint_guess: float32 [2, 20, 128, 1024], P(None, 'gz', 'gy', 'gx'), may hold values from -6 to 6
- viscosity: float32 [20, 128, 1024], P('gz', 'gy', 'gx'), may hold values from 0.2 to 2
- friction: float32 [128, 1024], P('gy', 'gx'), may hold values from 0.2 to 5
- base_velocity: float32 [2, 128, 1024], P(None, 'gy', 'gx'), may hold values from -6 to 6
- surface_slope: float32 [2, 128, 1024], P(None, 'gy', 'gx'), may hold values from -6 to 6
- ice_mask: int32 [128, 1024], P('gy', 'gx'), may hold values 0 or 1
- pixel_misfit: float32 [524288], P(('gx', 'gy', 'gz')), may hold values from -6 to 6
- pixel_look: float32 [524288], P(('gx', 'gy', 'gz')), may hold values from -3.140625 to 3.140625
- pixel_tile: int32 [524288, 1], P(('gx', 'gy', 'gz')), may hold values from 0 to 7; in each aligned block of 16384 rows (0 to 16383, 16384 to 32767, ...) at most 4096 rows name the same one
- pixel_cell: int32 [524288], P(('gx', 'gy', 'gz')), may hold values from 0 to 16383
- pixel_count: int32 [32], P(('gx', 'gy', 'gz')), may hold values from 1 to 16384, 393216 in all
Outputs:
- adjoint: float32 [2, 20, 128, 1024], P(None, 'gz', 'gy', 'gx')
- sensitivity_maps: float32 [2, 128, 1024], P(None, ('gy', 'gz'), 'gx')
Inputs may be any that keep to these rules, and one draw needn't show every extreme that they name: `pixel_tile`: among the rows of one device no tile is named more than 4096 times, a bound that some block reaches. `pixel_count`: rows of a device from its count on are padding.
All inputs are finite; a program needn't handle non-finite values. No bound on the sum of `ice_mask` on one device may be relied on, other than what follows from the above.
Results may differ from a plain program's by a relative error of at most 0.00002.
Values sent between devices are 32-bit elements; how exact they have to be, the bound alone decides.
A program may use at most 128 MiB of HBM per device.

v0:
```python
import jax
import jax.numpy as jnp
from jax import lax
from jax.sharding import PartitionSpec as P

ITERS = 2
OMEGA = 0.6
VERTICAL = 4.0


def padded_2(block, sides, width):
    for axis, dim in sides:
        count = lax.axis_size(axis)
        forward = [(i, i + 1) for i in range(count - 1)]
        backward = [(target, source) for source, target in forward]
        low = lax.ppermute(
            lax.slice_in_dim(block, block.shape[dim] - width, None, axis=dim), axis, forward
        )
        high = lax.ppermute(lax.slice_in_dim(block, 0, width, axis=dim), axis, backward)
        block = jnp.concatenate([low, block, high], axis=dim)
    return block


def box_apply(padded, visc_pad, mask_east, mask_north, mask_upper):
    first = padded[0]
    second = padded[1]
    base_a = first[:-1, :-1, :-1]
    base_b = second[:-1, :-1, :-1]
    east_a = (first[:-1, :-1, 1:] - base_a) * mask_east
    east_b = (second[:-1, :-1, 1:] - base_b) * mask_east
    north_a = (first[:-1, 1:, :-1] - base_a) * mask_north
    north_b = (second[:-1, 1:, :-1] - base_b) * mask_north
    upper_a = (first[1:, :-1, :-1] - base_a) * mask_upper
    upper_b = (second[1:, :-1, :-1] - base_b) * mask_upper
    visc_box = visc_pad[:-1, :-1, :-1]
    along_x = visc_box * (4.0 * east_a + 2.0 * north_b) * mask_east
    along_y = visc_box * (4.0 * north_b + 2.0 * east_a) * mask_north
    shear = visc_box * (north_a + east_b)
    shear_x = shear * mask_east
    shear_y = shear * mask_north
    vert_a = VERTICAL * visc_box * upper_a
    vert_b = VERTICAL * visc_box * upper_b
    result_a = (
        along_x[1:, 1:, :-1]
        - along_x[1:, 1:, 1:]
        + (shear_y[1:, :-1, 1:] - shear_y[1:, 1:, 1:])
        + (vert_a[:-1, 1:, 1:] - vert_a[1:, 1:, 1:])
    )
    result_b = (
        along_y[1:, :-1, 1:]
        - along_y[1:, 1:, 1:]
        + (shear_x[1:, 1:, :-1] - shear_x[1:, 1:, 1:])
        + (vert_b[:-1, 1:, 1:] - vert_b[1:, 1:, 1:])
    )
    return jnp.stack([result_a, result_b])


def body(
    adjoint_guess,
    viscosity,
    friction,
    base_velocity,
    surface_slope,
    ice_mask,
    pixel_misfit,
    pixel_look,
    pixel_tile,
    pixel_cell,
    pixel_count,
):
    layer_local = adjoint_guess.shape[1]
    rows_local = adjoint_guess.shape[2]
    cols_local = adjoint_guess.shape[3]
    count_x = lax.axis_size("gx")
    count_y = lax.axis_size("gy")
    count_z = lax.axis_size("gz")
    layer_total = layer_local * count_z
    full_x = cols_local * count_x
    full_y = rows_local * count_y
    tile_total = count_x * count_y
    per_device = pixel_misfit.shape[0]
    capacity = 2 * per_device // tile_total
    mask_float = ice_mask.astype(jnp.float32)
    live = jnp.arange(per_device, dtype=jnp.int32) < pixel_count[0]
    values = jnp.where(live, pixel_misfit, jnp.float32(0.0))
    dest_tile = pixel_tile[:, 0]
    one_hot = (dest_tile[:, None] == jnp.arange(tile_total, dtype=jnp.int32)[None, :]).astype(
        jnp.int32
    )
    running = jnp.cumsum(one_hot, axis=0)
    slot_index = jnp.sum(one_hot * running, axis=1) - 1
    position = dest_tile * capacity + slot_index
    payload = jnp.stack(
        [values * jnp.cos(pixel_look), values * jnp.sin(pixel_look), pixel_cell.astype(jnp.float32)]
    )
    outbox = jnp.zeros((3, tile_total * capacity), jnp.float32).at[:, position].set(payload)
    inbox = lax.all_to_all(
        outbox.reshape(3, tile_total, capacity),
        ("gx", "gy"),
        split_axis=1,
        concat_axis=1,
        tiled=True,
    )
    received = inbox.reshape(3, tile_total * capacity)
    cell_ids = received[2].astype(jnp.int32)
    forcing = jnp.zeros((2, rows_local * cols_local), jnp.float32).at[:, cell_ids].add(received[:2])
    forcing = forcing.reshape(2, rows_local, cols_local)
    forcing = lax.psum(forcing, "gz") * mask_float[None]
    layer_ids = lax.axis_index("gz") * layer_local + jnp.arange(layer_local, dtype=jnp.int32)
    bottom = (layer_ids == 0).astype(jnp.float32)[:, None, None]
    top = (layer_ids == layer_total - 1).astype(jnp.float32)[:, None, None]
    rhs = forcing[:, None, :, :] * top[None]
    basal = friction[None] * bottom
    damping = OMEGA / (18.0 * viscosity + basal)
    east_ids = lax.axis_index("gx") * cols_local + jnp.arange(cols_local + 1, dtype=jnp.int32) - 1
    north_ids = lax.axis_index("gy") * rows_local + jnp.arange(rows_local + 1, dtype=jnp.int32) - 1
    upper_ids = (
        lax.axis_index("gz") * layer_local + jnp.arange(layer_local + 1, dtype=jnp.int32) - 1
    )
    mask_east = (east_ids + 1 < full_x).astype(jnp.float32)[None, None, :]
    mask_north = (north_ids + 1 < full_y).astype(jnp.float32)[None, :, None]
    mask_upper = (upper_ids + 1 < layer_total).astype(jnp.float32)[:, None, None]
    adjoint = adjoint_guess
    for sweep in range(ITERS):
        stacked = jnp.concatenate([adjoint, viscosity[None]], axis=0)
        rims = padded_2(stacked, (("gx", 3), ("gy", 2), ("gz", 1)), 1)
        image = (
            box_apply(rims[:2], rims[2], mask_east, mask_north, mask_upper) + basal[None] * adjoint
        )
        adjoint = adjoint + damping[None] * (rhs - image)
    on_base = (lax.axis_index("gz") == 0).astype(jnp.float32)
    fric_term = (
        -on_base
        * mask_float
        * friction
        * (base_velocity[0] * adjoint[0, 0] + base_velocity[1] * adjoint[1, 0])
    )
    drive_term = (
        0.25
        * mask_float
        * jnp.sum(surface_slope[0][None] * adjoint[0] + surface_slope[1][None] * adjoint[1], axis=0)
    )
    maps = lax.psum_scatter(
        jnp.stack([fric_term, drive_term]), "gz", scatter_dimension=1, tiled=True
    )
    return (adjoint, maps)


def solution(mesh):
    return jax.shard_map(
        body,
        mesh=mesh,
        in_specs=(
            P(None, "gz", "gy", "gx"),
            P("gz", "gy", "gx"),
            P("gy", "gx"),
            P(None, "gy", "gx"),
            P(None, "gy", "gx"),
            P("gy", "gx"),
            P(("gx", "gy", "gz")),
            P(("gx", "gy", "gz")),
            P(("gx", "gy", "gz"), None),
            P(("gx", "gy", "gz")),
            P(("gx", "gy", "gz")),
        ),
        out_specs=(P(None, "gz", "gy", "gx"), P(None, ("gy", "gz"), "gx")),
        check_vma=False,
    )
```

profile of v0, /device:TPU:0, one launch (start us, length us, event | category | flops | bytes accessed | tf_op | source)
XLA Modules:
  0.0 580.0 jit_solution(1309384241617030706)
XLA Ops:
  7.2 2.4 fusion.57
  9.5 5.0 collective-permute-start
  14.5 1.3 collective-permute-start.1
  18.6 5.1 copy.28
  25.2 47.4 %scatter_custom_fusion = f32[3,32768]{0,1:T(8,128)} fusion(s32[16384]{0:T(1024)S(1)} %bitcast.116, f32[16384,3]{1,0:T(8,128)} %copy.28, f32[]{:T(128)} %constant.26.clone.1), kind=kCustom, calls=%fused_computation.2 | custom fusion | bytes 393728 | tf_op jit(solution)/shard_map/scatter | solution.py:96
  72.6 9.9 %copy.29 = f32[3,8,4096]{2,0,1:T(4,128)} copy(f32[3,8,4096]{0,2,1:T(8,128)} %bitcast.96) | data formatting | bytes 786432 | tf_op jit(solution)/shard_map/reshape | solution.py:98
  82.5 7.0 %all-to-all-start = ((f32[3,8,4096]{2,0,1:T(4,128)}), f32[3,8,4096]{2,0,1:T(4,128)S(1)}, u32[]{:S(2)}, u32[]{:S(2)}) async-start(f32[3,8,4096]{2,0,1:T(4,128)} %copy.29), calls=%async_computation | async-start | bytes 1048576 | tf_op jit(solution)/shard_map/all_to_all | solution.py:97
  90.3 3.9 collective-permute-start.2
  95.7 4.2 collective-permute-done.3
  100.6 1.3 collective-permute-start.4
  101.9 1.5 collective-permute-start.5
  103.6 3.6 collective-permute-done.5
  108.0 1.8 broadcast_multiply_fusion.2
  110.6 1.4 fusion.41
  112.1 8.3 %copy.30 = f32[32768,2]{1,0:T(8,128)} copy(f32[32768,2]{0,1:T(2,128)S(1)} %bitcast.107) | data formatting | bytes 524288 | tf_op jit(solution)/shard_map/slice | solution.py:106
  120.7 188.6 %scatter_custom_fusion.1 = f32[2,16384]{0,1:T(8,128)} fusion(s32[32768]{0:T(1024)S(1)} %bitcast.115, f32[32768,2]{1,0:T(8,128)} %copy.30, f32[]{:T(128)} %constant.26.clone.1), kind=kCustom, calls=%fused_computation.5 | custom fusion | flops 65536 | bytes 131584 | tf_op jit(solution)/shard_map/scatter-add | solution.py:106
  309.4 3.4 fusion.69
  312.8 182.0 %all-reduce.2.cloned.1.call-done = f32[2,64,256]{0,2,1:T(8,128)} async-done(((f32[2,64,256]{0,2,1:T(8,128)}), f32[2,64,256]{0,2,1:T(8,128)}) %all-reduce.2.cloned.1.call-update) | async-done | bytes 131088 | tf_op jit(solution)/shard_map/psum | solution.py:108
  494.8 7.9 %broadcast_multiply_fusion = f32[2,64,256]{0,2,1:T(8,128)} fusion(f32[2,64,256]{0,2,1:T(8,128)} %all-reduce.2.cloned.1.call-done, f32[64,256]{1,0:T(8,128)S(1)} %convert_element_type.67), kind=kLoop, calls=%fused_computation.4 | loop fusion | flops 32768 | bytes 327680 | tf_op jit(solution)/shard_map/mul | solution.py:108
  502.7 5.2 copy.31
  508.4 3.4 collective-permute-start.6
  511.8 1.3 collective-permute-start.7
  513.1 8.8 %collective-permute-done.6 = f32[3,5,64,1]{3,2,1,0:T(8,128)S(1)} collective-permute-done((f32[3,5,64,1]{3,2,1,0:T(8,128)S(1)}, f32[3,5,64,1]{3,2,1,0:T(8,128)S(1)}, u32[]{:S(2)}, u32[]{:S(2)}) %collective-permute-start.6) | collective-permute-done | bytes 3872 | tf_op jit(solution)/shard_map/ppermute | solution.py:16
  521.9 4.1 collective-permute-done.7
  527.3 4.0 collective-permute-start.8
  532.6 4.7 collective-permute-done.9
  537.3 1.4 fusion.23
  538.7 1.3 collective-permute-start.10
  540.0 1.5 collective-permute-start.11
  541.6 3.2 collective-permute-done.11
  544.8 1.4 fusion.15
  550.1 23.0 %reduce-scatter.2.cloned.1.call-done = f32[2,16,256]{2,1,0:T(8,128)} async-done(((f32[2,64,256]{2,1,0:T(8,128)}), f32[2,16,256]{2,1,0:T(8,128)}) %reduce-scatter.2.cloned.1.call-update) | async-done | bytes 32784 | tf_op jit(solution)/shard_map/reduce_scatter | solution.py:143
  (83 shorter events, 15.4 us)
Async XLA Ops:
  9.5 80.1 %collective-permute-start = (f32[3,5,64,1]{3,2,1,0:T(8,128)}, f32[3,5,64,1]{3,2,1,0:T(8,128)S(1)}, u32[]{:S(2)}, u32[]{:S(2)}) collective-permute-start(f32[3,5,64,1]{3,2,1,0:T(8,128)} %get-tuple-element.26), channel_id=1, source_target_pairs={{0,8},{8,16},{16,24},{1,9},{9,17},{17,25},{2,10},{10,18},{18,26},{... | collective-permute-start | bytes 11528 | tf_op jit(solution)/shard_map/ppermute | solution.py:16
  14.5 75.2 %collective-permute-start.1 = (f32[3,5,64,1]{3,2,1,0:T(8,128)}, f32[3,5,64,1]{3,2,1,0:T(8,128)S(1)}, u32[]{:S(2)}, u32[]{:S(2)}) collective-permute-start(f32[3,5,64,1]{3,2,1,0:T(8,128)} %get-tuple-element.27), channel_id=1, source_target_pairs={{8,0},{16,8},{24,16},{9,1},{17,9},{25,17},{10,2},{18,10},{26,18},{... | collective-permute-start | bytes 11528 | tf_op jit(solution)/shard_map/ppermute | solution.py:19
  18.6 5.1 copy-start.7
  72.6 17.1 %copy-start = (f32[5,64,256]{2,1,0:T(8,128)S(1)}, f32[5,64,256]{2,1,0:T(8,128)}, u32[]{:S(2)}) copy-start(f32[5,64,256]{2,1,0:T(8,128)} %param.12) | copy-start | bytes 983044
  72.6 17.1 %copy-start.1 = (f32[2,5,64,256]{3,2,1,0:T(8,128)S(1)}, f32[2,5,64,256]{3,2,1,0:T(8,128)}, u32[]{:S(2)}) copy-start(f32[2,5,64,256]{3,2,1,0:T(8,128)} %param.11) | copy-start | bytes 1966084
  82.5 13.0 %copy-start.8 = (s32[64,256]{1,0:T(8,128)S(1)}, s32[64,256]{1,0:T(8,128)}, u32[]{:S(2)}) copy-start(s32[64,256]{1,0:T(8,128)} %param.16) | copy-start | bytes 196612
  82.5 29.5 %all-to-all-start = ((f32[3,8,4096]{2,0,1:T(4,128)}), f32[3,8,4096]{2,0,1:T(4,128)S(1)}, u32[]{:S(2)}, u32[]{:S(2)}) async-start(f32[3,8,4096]{2,0,1:T(4,128)} %copy.29), calls=%async_computation | async-start | bytes 1048576 | tf_op jit(solution)/shard_map/all_to_all | solution.py:97
  89.5 405.3 %all-reduce.2.cloned.1.call-start = ((), (), s32[]{:S(2)}) async-start(), calls=%async_computation.2 | async-start | bytes 16777216 | tf_op jit(solution)/shard_map/psum | solution.py:108
  90.3 5.4 collective-permute-start.2
  94.2 5.7 collective-permute-start.3
  95.5 7.9 %copy-start.9 = (f32[64,256]{1,0:T(8,128)S(1)}, f32[64,256]{1,0:T(8,128)}, u32[]{:S(2)}) copy-start(f32[64,256]{1,0:T(8,128)} %param.13) | copy-start | bytes 196612
  100.6 3.0 collective-permute-start.4
  101.9 5.2 collective-permute-start.5
  103.5 404.4 %copy-start.3 = (f32[5,64,256]{2,1,0:T(8,128)}, f32[5,64,256]{2,1,0:T(8,128)S(1)}, u32[]{:S(2)}) copy-start(f32[5,64,256]{2,1,0:T(8,128)S(1)} %get-tuple-element.36) | copy-start | bytes 983044
  103.6 404.4 %copy-start.5 = (f32[5,64,256]{2,1,0:T(8,128)}, f32[5,64,256]{2,1,0:T(8,128)S(1)}, u32[]{:S(2)}) copy-start(f32[5,64,256]{2,1,0:T(8,128)S(1)} %get-tuple-element.37) | copy-start | bytes 983044
  309.3 263.8 %reduce-scatter.2.cloned.1.call-start = ((), (), s32[]{:S(2)}) async-start(), calls=%async_computation.3 | async-start | bytes 163840 | tf_op jit(solution)/shard_map/reduce_scatter | solution.py:143
  508.4 13.5 %collective-permute-start.6 = (f32[3,5,64,1]{3,2,1,0:T(8,128)S(1)}, f32[3,5,64,1]{3,2,1,0:T(8,128)S(1)}, u32[]{:S(2)}, u32[]{:S(2)}) collective-permute-start(f32[3,5,64,1]{3,2,1,0:T(8,128)S(1)} %get-tuple-element.24), channel_id=1, source_target_pairs={{0,8},{8,16},{16,24},{1,9},{9,17},{17,25},{2,10},{10,18},{18,26},{... | collective-permute-start | bytes 11528 | tf_op jit(solution)/shard_map/ppermute | solution.py:16
  511.8 14.3 %collective-permute-start.7 = (f32[3,5,64,1]{3,2,1,0:T(8,128)S(1)}, f32[3,5,64,1]{3,2,1,0:T(8,128)S(1)}, u32[]{:S(2)}, u32[]{:S(2)}) collective-permute-start(f32[3,5,64,1]{3,2,1,0:T(8,128)S(1)} %get-tuple-element.25), channel_id=1, source_target_pairs={{8,0},{16,8},{24,16},{9,1},{17,9},{25,17},{10,2},{18,10},{26,18},{... | collective-permute-start | bytes 11528 | tf_op jit(solution)/shard_map/ppermute | solution.py:19
  527.3 5.3 collective-permute-start.8
  531.2 6.0 %collective-permute-start.9 = (f32[3,5,1,258]{3,2,1,0:T(1,128)}, f32[3,5,1,258]{3,2,1,0:T(1,128)}, u32[]{:S(2)}, u32[]{:S(2)}) collective-permute-start(f32[3,5,1,258]{3,2,1,0:T(1,128)} %get-tuple-element.21), channel_id=1, source_target_pairs={{4,0},{5,1},{6,2},{7,3},{12,8},{13,9},{14,10},{15,11},{20,16},{21,... | collective-permute-start | bytes 46448 | tf_op jit(solution)/shard_map/ppermute | solution.py:19
  532.5 9.0 %copy-start.10 = (f32[2,64,256]{2,1,0:T(8,128)S(1)}, f32[2,64,256]{2,1,0:T(8,128)}, u32[]{:S(2)}) copy-start(f32[2,64,256]{2,1,0:T(8,128)} %param.15) | copy-start | bytes 393220
  538.7 2.9 collective-permute-start.10
  540.0 4.7 collective-permute-start.11
  547.4 1.1 copy-start.4
  547.4 1.1 copy-start.6
  548.5 0.9 copy-start.11
  548.8 24.3 %copy-start.2 = (f32[2,5,64,256]{3,2,1,0:T(8,128)}, f32[2,5,64,256]{3,2,1,0:T(8,128)S(1)}, u32[]{:S(2)}) copy-start(f32[2,5,64,256]{3,2,1,0:T(8,128)S(1)} %fusion.51) | copy-start | bytes 1966084
Sparse Core Ops, SparseCore 0:
  309.4 185.3 all-reduce.1
  550.2 22.8 reduce-scatter.1
where the time goes:
time: 581 us; the launch traced here: 580 us
  waiting for transfers between devices  234 us (40%)
  other arithmetic  219 us (38%)
  local copies, waits for them, and re-layouts  78 us (13%)
  starting transfers between devices  34.1 us (6%)
  between operations  15.2 us (3%)
    scatter-add x1, other arithmetic, body(): jnp.zeros((2, rows_local * cols_local), jnp.float32).at[:, cell_ids]  189 us
    psum x1, waiting for transfers between devices, body(): forcing = lax.psum(forcing, 'gz') * mask_float[None]  182 us
    scatter x1, local copies, waits for them, and re-layouts, body(): jnp.zeros((3, tile_total * capacity), jnp.float32).at[:, position]  47.4 us
    reduce_scatter x1, waiting for transfers between devices, body(): lax.psum_scatter(jnp.stack([fric_term, drive_term]), 'gz', scatter_dimens...  23 us
    ppermute x6, waiting for transfers between devices, padded_2(): lax.ppermute(lax.slice_in_dim(block, 0, width, axis=dim), axis, backward)  19.8 us
    ppermute x6, starting transfers between devices, padded_2(): lax.ppermute(lax.slice_in_dim(block, block.shape[dim] - width, None, axis...  18.9 us
  transfers between devices with their start and end apart: 15, of which 9 were waited for; matrix products, arithmetic and copies ran while one was open for 13% of the time, Pallas kernels for 0%

commit v1 on v0

--- a/solution.py
+++ b/solution.py
@@ -105,7 +105,7 @@
     cell_ids = received[2].astype(jnp.int32)
     forcing = jnp.zeros((2, rows_local * cols_local), jnp.float32).at[:, cell_ids].add(received[:2])
     forcing = forcing.reshape(2, rows_local, cols_local)
-    forcing = lax.psum(forcing, "gz") * mask_float[None]
+    forcing = jnp.sum(lax.all_gather(forcing, "gz"), axis=0) * mask_float[None]
     layer_ids = lax.axis_index("gz") * layer_local + jnp.arange(layer_local, dtype=jnp.int32)
     bottom = (layer_ids == 0).astype(jnp.float32)[:, None, None]
     top = (layer_ids == layer_total - 1).astype(jnp.float32)[:, None, None]

time: 581 us -> 442 us (0.76)
  waiting for transfers between devices: 234 us -> 53.7 us
  starting transfers between devices: 34.1 us -> 59 us
  local copies, waits for them, and re-layouts: 78 us -> 89 us
  blocking collectives: 0 us -> 10.7 us
  other arithmetic: 219 us -> 213 us
    psum x1 -> x0, waiting for transfers between devices: 182 us -> none  [body(): forcing = lax.psum(forcing, 'gz') * mask_float[None]]
    ppermute x6, starting transfers between devices: 18.9 us -> 43.8 us  [padded_2(): lax.ppermute(lax.slice_in_dim(block, block.shape[dim] - width, None, axis...]
    all_gather x0 -> x1, blocking collectives: none -> 10.7 us  [body(): forcing = jnp.sum(lax.all_gather(forcing, 'gz'), axis=0) * mask_float[None]]
  transfers between devices with their start and end apart: 15 -> 14, of which waited for: 9 -> 9; matrix products, arithmetic and copies ran while one was open for 13% -> 16% of each run, Pallas kernels for 0% -> 0%
where the time goes in v1:
time: 442 us; the launch traced here: 441 us
  other arithmetic  213 us (48%)
  local copies, waits for them, and re-layouts  89 us (20%)
  starting transfers between devices  59 us (13%)
  waiting for transfers between devices  53.7 us (12%)
  between operations  15.3 us (3%)
  blocking collectives  10.7 us (2%)
    scatter-add x1, other arithmetic, body(): jnp.zeros((2, rows_local * cols_local), jnp.float32).at[:, cell_ids]  189 us
    scatter x1, local copies, waits for them, and re-layouts, body(): jnp.zeros((3, tile_total * capacity), jnp.float32).at[:, position]  47.4 us
    ppermute x6, starting transfers between devices, padded_2(): lax.ppermute(lax.slice_in_dim(block, block.shape[dim] - width, None, axis...  43.8 us
    reduce_scatter x1, waiting for transfers between devices, body(): lax.psum_scatter(jnp.stack([fric_term, drive_term]), 'gz', scatter_dimens...  24.1 us
    ppermute x6, waiting for transfers between devices, padded_2(): lax.ppermute(lax.slice_in_dim(block, 0, width, axis=dim), axis, backward)  19.4 us
    all_gather x1, blocking collectives, body(): forcing = jnp.sum(lax.all_gather(forcing, 'gz'), axis=0) * mask_float[None]  10.7 us
    ppermute x6, waiting for transfers between devices, padded_2(): lax.ppermute(lax.slice_in_dim(block, block.shape[dim] - width, None, axis...  10.2 us
    reshape x1, local copies, waits for them, and re-layouts, body(): outbox.reshape(3, tile_total, capacity)  9.94 us
  transfers between devices with their start and end apart: 14, of which 9 were waited for; matrix products, arithmetic and copies ran while one was open for 16% of the time, Pallas kernels for 0%

profile of v1, /device:TPU:0, one launch (start us, length us, event | category | flops | bytes accessed | tf_op | source)
XLA Modules:
  0.0 440.9 jit_solution(14025563960086484744)
XLA Ops:
  7.2 1.4 fusion.57
  8.5 5.0 %collective-permute-start = (f32[3,5,64,1]{3,2,1,0:T(8,128)S(1)}, f32[3,5,64,1]{3,2,1,0:T(8,128)S(1)}, u32[]{:S(2)}, u32[]{:S(2)}) collective-permute-start(f32[3,5,64,1]{3,2,1,0:T(8,128)S(1)} %get-tuple-element.26), channel_id=1, source_target_pairs={{0,8},{8,16},{16,24},{1,9},{9,17},{17,25},{2,10},{10,18},{18,26},{... | collective-permute-start | bytes 11528 | tf_op jit(solution)/shard_map/ppermute | solution.py:16
  13.5 1.3 collective-permute-start.1
  17.6 5.1 %copy.28 = f32[16384,3]{1,0:T(8,128)} copy(f32[16384,3]{0,1:T(4,128)S(1)} %maximum_bitcast_fusion) | data formatting | bytes 393216 | tf_op jit(solution)/shard_map/stack | solution.py:93
  24.2 47.4 %scatter_custom_fusion = f32[3,32768]{0,1:T(8,128)} fusion(s32[16384]{0:T(1024)S(1)} %bitcast.116, f32[16384,3]{1,0:T(8,128)} %copy.28, f32[]{:T(128)} %constant.26.clone.1), kind=kCustom, calls=%fused_computation.2 | custom fusion | bytes 393728 | tf_op jit(solution)/shard_map/scatter | solution.py:96
  71.6 9.9 %copy.29 = f32[3,8,4096]{2,0,1:T(4,128)} copy(f32[3,8,4096]{0,2,1:T(8,128)} %bitcast.96) | data formatting | bytes 786432 | tf_op jit(solution)/shard_map/reshape | solution.py:98
  81.5 7.0 %all-to-all-start = ((f32[3,8,4096]{2,0,1:T(4,128)}), f32[3,8,4096]{2,0,1:T(4,128)}, u32[]{:S(2)}, u32[]{:S(2)}) async-start(f32[3,8,4096]{2,0,1:T(4,128)} %copy.29), calls=%async_computation | async-start | bytes 1048576 | tf_op jit(solution)/shard_map/all_to_all | solution.py:97
  89.8 3.9 collective-permute-start.2
  93.7 1.3 collective-permute-start.3
  95.2 4.2 collective-permute-done.3
  100.1 1.3 collective-permute-start.4
  101.4 1.5 collective-permute-start.5
  103.1 3.6 collective-permute-done.5
  110.7 8.3 %copy.30 = f32[32768,2]{1,0:T(8,128)} copy(f32[32768,2]{0,1:T(2,128)S(1)} %bitcast.107) | data formatting | bytes 524288 | tf_op jit(solution)/shard_map/slice | solution.py:106
  120.3 188.6 %scatter_custom_fusion.1 = f32[2,16384]{0,1:T(8,128)} fusion(s32[32768]{0:T(1024)S(1)} %bitcast.115, f32[32768,2]{1,0:T(8,128)} %copy.30, f32[]{:T(128)} %constant.26.clone.1), kind=kCustom, calls=%fused_computation.5 | custom fusion | flops 65536 | bytes 131584 | tf_op jit(solution)/shard_map/scatter-add | solution.py:106
  308.9 5.2 %copy.31 = f32[1,2,64,256]{3,2,1,0:T(8,128)S(1)} copy(f32[1,2,64,256]{1,3,2,0:T(8,128)} %bitcast.97) | data formatting | bytes 262144 | tf_op jit(solution)/shard_map/all_gather;reshape | solution.py:108
  314.1 10.7 %all_gather.3 = f32[4,2,64,256]{3,2,1,0:T(8,128)S(1)} all-gather(f32[1,2,64,256]{3,2,1,0:T(8,128)S(1)} %copy.31), channel_id=1, replica_groups=mesh['gx'=4,'gy'=2,'gz'=4] {'gz'}, dimensions={0}, use_global_device_ids=true | all-gather | bytes 655360 | tf_op jit(solution)/shard_map/all_gather | solution.py:108
  324.8 4.7 %copy.34 = f32[2,64,256]{0,2,1:T(8,128)} copy(f32[2,64,256]{2,1,0:T(8,128)S(1)} %reduce_sum.28) | data formatting | bytes 262144
  329.5 8.0 %broadcast_multiply_fusion = f32[2,64,256]{0,2,1:T(8,128)} fusion(f32[2,64,256]{0,2,1:T(8,128)} %copy.34, f32[64,256]{1,0:T(8,128)S(1)} %convert_element_type.67), kind=kLoop, calls=%fused_computation.4 | loop fusion | flops 32768 | bytes 327680 | tf_op jit(solution)/shard_map/mul | solution.py:108
  337.5 5.2 %copy.33 = f32[2,64,256]{2,1,0:T(8,128)S(1)} copy(f32[2,64,256]{0,2,1:T(8,128)} %broadcast_multiply_fusion) | data formatting | bytes 262144 | tf_op jit(solution)/shard_map/mul | solution.py:108
  343.1 31.0 %collective-permute-start.6 = (f32[3,5,64,1]{3,2,1,0:T(8,128)S(1)}, f32[3,5,64,1]{3,2,1,0:T(8,128)S(1)}, u32[]{:S(2)}, u32[]{:S(2)}) collective-permute-start(f32[3,5,64,1]{3,2,1,0:T(8,128)S(1)} %get-tuple-element.24), channel_id=1, source_target_pairs={{0,8},{8,16},{16,24},{1,9},{9,17},{17,25},{2,10},{10,18},{18,26},{... | collective-permute-start | bytes 11528 | tf_op jit(solution)/shard_map/ppermute | solution.py:16
  374.2 1.3 collective-permute-start.7
  375.5 9.6 %collective-permute-done.6 = f32[3,5,64,1]{3,2,1,0:T(8,128)S(1)} collective-permute-done((f32[3,5,64,1]{3,2,1,0:T(8,128)S(1)}, f32[3,5,64,1]{3,2,1,0:T(8,128)S(1)}, u32[]{:S(2)}, u32[]{:S(2)}) %collective-permute-start.6) | collective-permute-done | bytes 3872 | tf_op jit(solution)/shard_map/ppermute | solution.py:16
  385.1 4.1 collective-permute-done.7
  390.5 1.3 collective-permute-start.8
  391.8 1.3 collective-permute-start.9
  393.5 4.2 collective-permute-done.9
  398.4 1.3 collective-permute-start.10
  399.8 1.5 collective-permute-start.11
  401.3 3.3 collective-permute-done.11
  404.6 1.4 fusion.15
  410.0 24.1 %reduce-scatter.2.cloned.1.call-done = f32[2,16,256]{2,1,0:T(8,128)} async-done(((f32[2,64,256]{2,1,0:T(8,128)}), f32[2,16,256]{2,1,0:T(8,128)}) %reduce-scatter.2.cloned.1.call-update) | async-done | bytes 32784 | tf_op jit(solution)/shard_map/reduce_scatter | solution.py:143
  (91 shorter events, 17.6 us)
Async XLA Ops:
  8.5 80.6 %collective-permute-start = (f32[3,5,64,1]{3,2,1,0:T(8,128)S(1)}, f32[3,5,64,1]{3,2,1,0:T(8,128)S(1)}, u32[]{:S(2)}, u32[]{:S(2)}) collective-permute-start(f32[3,5,64,1]{3,2,1,0:T(8,128)S(1)} %get-tuple-element.26), channel_id=1, source_target_pairs={{0,8},{8,16},{16,24},{1,9},{9,17},{17,25},{2,10},{10,18},{18,26},{... | collective-permute-start | bytes 11528 | tf_op jit(solution)/shard_map/ppermute | solution.py:16
  13.5 75.6 %collective-permute-start.1 = (f32[3,5,64,1]{3,2,1,0:T(8,128)S(1)}, f32[3,5,64,1]{3,2,1,0:T(8,128)S(1)}, u32[]{:S(2)}, u32[]{:S(2)}) collective-permute-start(f32[3,5,64,1]{3,2,1,0:T(8,128)S(1)} %get-tuple-element.27), channel_id=1, source_target_pairs={{8,0},{16,8},{24,16},{9,1},{17,9},{25,17},{10,2},{18,10},{26,18},{... | collective-permute-start | bytes 11528 | tf_op jit(solution)/shard_map/ppermute | solution.py:19
  17.6 5.1 %copy-start.7 = (s32[16384,1]{0,1:T(1,128)S(1)}, s32[16384,1]{0,1:T(1,128)}, u32[]{:S(2)}) copy-start(s32[16384,1]{0,1:T(1,128)} %param.19) | copy-start | bytes 196612
  71.6 17.6 %copy-start = (f32[5,64,256]{2,1,0:T(8,128)S(1)}, f32[5,64,256]{2,1,0:T(8,128)}, u32[]{:S(2)}) copy-start(f32[5,64,256]{2,1,0:T(8,128)} %param.12) | copy-start | bytes 983044
  71.6 17.6 %copy-start.1 = (f32[2,5,64,256]{3,2,1,0:T(8,128)S(1)}, f32[2,5,64,256]{3,2,1,0:T(8,128)}, u32[]{:S(2)}) copy-start(f32[2,5,64,256]{3,2,1,0:T(8,128)} %param.11) | copy-start | bytes 1966084
  81.5 13.5 %copy-start.8 = (s32[64,256]{1,0:T(8,128)S(1)}, s32[64,256]{1,0:T(8,128)}, u32[]{:S(2)}) copy-start(s32[64,256]{1,0:T(8,128)} %param.16) | copy-start | bytes 196612
  81.5 28.0 %all-to-all-start = ((f32[3,8,4096]{2,0,1:T(4,128)}), f32[3,8,4096]{2,0,1:T(4,128)}, u32[]{:S(2)}, u32[]{:S(2)}) async-start(f32[3,8,4096]{2,0,1:T(4,128)} %copy.29), calls=%async_computation | async-start | bytes 1048576 | tf_op jit(solution)/shard_map/all_to_all | solution.py:97
  88.6 345.5 %reduce-scatter.2.cloned.1.call-start = ((), (), s32[]{:S(2)}) async-start(), calls=%async_computation.2 | async-start | bytes 163840 | tf_op jit(solution)/shard_map/reduce_scatter | solution.py:143
  89.8 5.4 %collective-permute-start.2 = (f32[3,5,1,258]{3,2,1,0:T(1,128)S(1)}, f32[3,5,1,258]{3,2,1,0:T(1,128)S(1)}, u32[]{:S(2)}, u32[]{:S(2)}) collective-permute-start(f32[3,5,1,258]{3,2,1,0:T(1,128)S(1)} %get-tuple-element.22), channel_id=1, source_target_pairs={{0,4},{1,5},{2,6},{3,7},{8,12},{9,13},{10,14},{11,15},{16,20},{17,... | collective-permute-start | bytes 46448 | tf_op jit(solution)/shard_map/ppermute | solution.py:16
  93.7 5.7 %collective-permute-start.3 = (f32[3,5,1,258]{3,2,1,0:T(1,128)S(1)}, f32[3,5,1,258]{3,2,1,0:T(1,128)S(1)}, u32[]{:S(2)}, u32[]{:S(2)}) collective-permute-start(f32[3,5,1,258]{3,2,1,0:T(1,128)S(1)} %get-tuple-element.23), channel_id=1, source_target_pairs={{4,0},{5,1},{6,2},{7,3},{12,8},{13,9},{14,10},{15,11},{20,16},{21,... | collective-permute-start | bytes 46448 | tf_op jit(solution)/shard_map/ppermute | solution.py:19
  95.0 7.9 %copy-start.9 = (f32[64,256]{1,0:T(8,128)S(1)}, f32[64,256]{1,0:T(8,128)}, u32[]{:S(2)}) copy-start(f32[64,256]{1,0:T(8,128)} %param.13) | copy-start | bytes 196612
  95.0 7.9 %copy-start.15 = (f32[5]{0:T(128)S(1)}, f32[5]{0:T(128)}, u32[]{:S(2)}) copy-start(f32[5]{0:T(128)} %get-tuple-element.41) | copy-start | bytes 64
  100.1 3.0 collective-permute-start.4
  101.4 5.2 %collective-permute-start.5 = (f32[3,1,66,258]{3,2,1,0:T(8,128)S(1)}, f32[3,1,66,258]{3,2,1,0:T(8,128)S(1)}, u32[]{:S(2)}, u32[]{:S(2)}) collective-permute-start(f32[3,1,66,258]{3,2,1,0:T(8,128)S(1)} %get-tuple-element.19), channel_id=1, source_target_pairs={{1,0},{2,1},{3,2},{5,4},{6,5},{7,6},{9,8},{10,9},{11,10},{13,12},{... | collective-permute-start | bytes 613016 | tf_op jit(solution)/shard_map/ppermute | solution.py:19
  103.1 239.6 %copy-start.3 = (f32[5,64,256]{2,1,0:T(8,128)}, f32[5,64,256]{2,1,0:T(8,128)S(1)}, u32[]{:S(2)}) copy-start(f32[5,64,256]{2,1,0:T(8,128)S(1)} %get-tuple-element.36) | copy-start | bytes 983044
  103.1 239.6 %copy-start.5 = (f32[5,64,256]{2,1,0:T(8,128)}, f32[5,64,256]{2,1,0:T(8,128)S(1)}, u32[]{:S(2)}) copy-start(f32[5,64,256]{2,1,0:T(8,128)S(1)} %get-tuple-element.37) | copy-start | bytes 983044
  343.1 42.0 %collective-permute-start.6 = (f32[3,5,64,1]{3,2,1,0:T(8,128)S(1)}, f32[3,5,64,1]{3,2,1,0:T(8,128)S(1)}, u32[]{:S(2)}, u32[]{:S(2)}) collective-permute-start(f32[3,5,64,1]{3,2,1,0:T(8,128)S(1)} %get-tuple-element.24), channel_id=1, source_target_pairs={{0,8},{8,16},{16,24},{1,9},{9,17},{17,25},{2,10},{10,18},{18,26},{... | collective-permute-start | bytes 11528 | tf_op jit(solution)/shard_map/ppermute | solution.py:16
  374.2 15.1 %collective-permute-start.7 = (f32[3,5,64,1]{3,2,1,0:T(8,128)S(1)}, f32[3,5,64,1]{3,2,1,0:T(8,128)S(1)}, u32[]{:S(2)}, u32[]{:S(2)}) collective-permute-start(f32[3,5,64,1]{3,2,1,0:T(8,128)S(1)} %get-tuple-element.25), channel_id=1, source_target_pairs={{8,0},{16,8},{24,16},{9,1},{17,9},{25,17},{10,2},{18,10},{26,18},{... | collective-permute-start | bytes 11528 | tf_op jit(solution)/shard_map/ppermute | solution.py:19
  390.5 3.0 collective-permute-start.8
  391.8 5.9 %collective-permute-start.9 = (f32[3,5,1,258]{3,2,1,0:T(1,128)}, f32[3,5,1,258]{3,2,1,0:T(1,128)S(1)}, u32[]{:S(2)}, u32[]{:S(2)}) collective-permute-start(f32[3,5,1,258]{3,2,1,0:T(1,128)} %get-tuple-element.21), channel_id=1, source_target_pairs={{4,0},{5,1},{6,2},{7,3},{12,8},{13,9},{14,10},{15,11},{20,16},{21,... | collective-permute-start | bytes 46448 | tf_op jit(solution)/shard_map/ppermute | solution.py:19
  393.1 8.2 %copy-start.11 = (f32[2,64,256]{2,1,0:T(8,128)S(1)}, f32[2,64,256]{2,1,0:T(8,128)}, u32[]{:S(2)}) copy-start(f32[2,64,256]{2,1,0:T(8,128)} %param.15) | copy-start | bytes 393220
  393.5 4.9 %copy-start.13 = (f32[3,5,1,258]{3,2,1,0:T(1,128)}, f32[3,5,1,258]{3,2,1,0:T(1,128)S(1)}, u32[]{:S(2)}) copy-start(f32[3,5,1,258]{3,2,1,0:T(1,128)S(1)} %collective-permute-done.8) | copy-start | bytes 46444
  397.7 0.7 copy-start.14
  398.4 2.9 collective-permute-start.10
  399.8 4.8 %collective-permute-start.11 = (f32[3,1,66,258]{3,2,1,0:T(8,128)S(1)}, f32[3,1,66,258]{3,2,1,0:T(8,128)S(1)}, u32[]{:S(2)}, u32[]{:S(2)}) collective-permute-start(f32[3,1,66,258]{3,2,1,0:T(8,128)S(1)} %get-tuple-element.17), channel_id=1, source_target_pairs={{1,0},{2,1},{3,2},{5,4},{6,5},{7,6},{9,8},{10,9},{11,10},{13,12},{... | collective-permute-start | bytes 613016 | tf_op jit(solution)/shard_map/ppermute | solution.py:19
  407.2 1.1 copy-start.4
  407.2 1.1 copy-start.6
  408.3 0.8 copy-start.10
  408.3 0.9 copy-start.12
  408.6 25.4 %copy-start.2 = (f32[2,5,64,256]{3,2,1,0:T(8,128)}, f32[2,5,64,256]{3,2,1,0:T(8,128)S(1)}, u32[]{:S(2)}) copy-start(f32[2,5,64,256]{3,2,1,0:T(8,128)S(1)} %fusion.51) | copy-start | bytes 1966084
Sparse Core Ops, SparseCore 0:
  410.1 23.8 reduce-scatter.1
